TPU v7x, 32 devices: a whole 2x2x4 slice. The times are simulated.
32 devices in a mesh: dp: 4 (over y, x), expert: 8 (over z, core).
Axes of the slice: x: 2, y: 2, z: 4, core: 2. Of those that a mesh axis runs over, the one named last changes fastest.
Arguments:
- tokens: bfloat16 [5120, 1024], P(('dp', 'expert')), may hold values from -6 to 6
- expert_ids: int32 [5120, 2], P(('dp', 'expert')), may hold values from 0 to 15, all different within a row; in each aligned block of 160 rows (0 to 159, 160 to 319, ...) at most 40 rows name the same one
- router: bfloat16 [1024, 16], replicated, may hold values from -0.5 to 0.5
- gate_up_weight: bfloat16 [16, 1024, 2048], P('expert', 'dp'), may hold values from -0.1875 to 0.1875
- down_weight: bfloat16 [16, 1024, 1024], P('expert', 'dp'), may hold values from -0.1875 to 0.1875
- out_grad: bfloat16 [5120, 1024], P(('dp', 'expert')), may hold values from -6 to 6
Outputs:
- mixed_out: bfloat16 [5120, 1024], P(('dp', 'expert'))
- tokens_grad: bfloat16 [5120, 1024], P(('dp', 'expert'))
- router_grad: float32 [1024, 16], replicated
- gate_up_grad: float32 [16, 1024, 2048], P('expert', 'dp')
- down_grad: float32 [16, 1024, 1024], P('expert', 'dp')
Inputs may be any that keep to these rules, and one draw needn't show every extreme that they name: `expert_ids`: the 2 experts of a token differ. Among the 160 tokens of one device no expert is named more than 40 times, and in every draw some expert is named exactly 40 times by the tokens of some device.
All inputs are finite; a program needn't handle non-finite values.
Results may differ from a plain program's by a relative error of at most 0.013.
Values may be sent and summed in bfloat16 or wider, within the bound.
A program may use at most 128 MiB of HBM per device.

v0:
```python
import jax
import jax.numpy as jnp
from jax import lax
from jax.sharding import PartitionSpec as P


def activate(gate_up, hidden_units):
    gate_part = gate_up[..., :hidden_units]
    up_part = gate_up[..., hidden_units:]
    sigmoid_gate = jax.nn.sigmoid(gate_part)
    active = gate_part * sigmoid_gate
    return ((active * up_part).astype(jnp.bfloat16), gate_part, up_part, sigmoid_gate, active)


def finish_rows(gate_up, full_down):
    hidden = activate(gate_up, full_down.shape[1])[0]
    produced = jnp.einsum(
        "sjcf,jfd->sjcd", hidden, full_down, preferred_element_type=jnp.float32
    ).astype(jnp.bfloat16)
    return lax.all_to_all(produced, "expert", split_axis=0, concat_axis=0, tiled=True)


def on_device(tokens, expert_ids, router, gate_up_weight, down_weight, out_grad):
    full_gate_up, full_down = (
        lax.all_gather(gate_up_weight, "dp", axis=1, tiled=True),
        lax.all_gather(down_weight, "dp", axis=1, tiled=True),
    )
    token_rows = tokens.shape[0]
    feature_dim = tokens.shape[1]
    pair_count = expert_ids.shape[1]
    owners = lax.axis_size("expert")
    local_count = full_gate_up.shape[0]
    experts = owners * local_count
    capacity = 2 * pair_count * token_rows // experts
    hidden_units = full_down.shape[1]
    slot_total = experts * capacity
    onehot = (expert_ids[:, :, None] == jnp.arange(experts, dtype=jnp.int32)[None, None, :]).astype(
        jnp.int32
    )
    per_token = jnp.sum(onehot, axis=1)
    before = jnp.cumsum(per_token, axis=0) - per_token
    position = jnp.sum(before[:, None, :] * onehot, axis=2)
    slot_index = expert_ids * capacity + position
    select = (
        slot_index[:, :, None] == jnp.arange(slot_total, dtype=jnp.int32)[None, None, :]
    ).astype(jnp.bfloat16)
    dispatch = select[:, 0, :] + select[:, 1, :]
    send_rows = jnp.dot(dispatch.T, tokens, preferred_element_type=jnp.float32).astype(jnp.bfloat16)
    send_rows = send_rows.reshape(owners, local_count, capacity, feature_dim)
    logits = jnp.dot(tokens, router, preferred_element_type=jnp.float32)
    onehot_float = onehot.astype(jnp.float32)
    chosen = jnp.sum(logits[:, None, :] * onehot_float, axis=2)
    gate_first = jax.nn.sigmoid(chosen[:, 0] - chosen[:, 1])
    gate_pair = jnp.stack([gate_first, 1.0 - gate_first], axis=1)
    received = lax.all_to_all(send_rows, "expert", split_axis=0, concat_axis=0, tiled=True)
    gate_up = jnp.einsum(
        "sjcd,jdf->sjcf", received, full_gate_up, preferred_element_type=jnp.float32
    )
    returned = finish_rows(gate_up, full_down)
    returned_flat = returned.reshape(slot_total, feature_dim)
    expert_out = jnp.einsum(
        "tks,sd->tkd", select, returned_flat, preferred_element_type=jnp.float32
    )
    mixed_out = jnp.sum(gate_pair[:, :, None] * expert_out, axis=1).astype(jnp.bfloat16)
    grad_float = out_grad.astype(jnp.float32)
    gate_grads = jnp.sum(grad_float[:, None, :] * expert_out, axis=2)
    common = gate_pair[:, 0] * gate_pair[:, 1] * (gate_grads[:, 0] - gate_grads[:, 1])
    logit_grads = common[:, None] * (onehot_float[:, 0, :] - onehot_float[:, 1, :])
    scaled = (gate_pair[:, :, None] * grad_float[:, None, :]).astype(jnp.bfloat16)
    grad_send = jnp.einsum(
        "tks,tkd->sd", select, scaled, preferred_element_type=jnp.float32
    ).astype(jnp.bfloat16)
    grad_send = grad_send.reshape(owners, local_count, capacity, feature_dim)
    grad_recv = lax.all_to_all(grad_send, "expert", split_axis=0, concat_axis=0, tiled=True)
    hidden, gate_part, up_part, sigmoid_gate, active = activate(gate_up, hidden_units)
    hidden_grad = jnp.einsum(
        "sjcd,jfd->sjcf", grad_recv, full_down, preferred_element_type=jnp.float32
    )
    gate_grad = hidden_grad * up_part * sigmoid_gate * (1.0 + gate_part * (1.0 - sigmoid_gate))
    up_grad = hidden_grad * active
    pre_grad = jnp.concatenate([gate_grad, up_grad], axis=3).astype(jnp.bfloat16)
    input_grad = jnp.einsum(
        "sjcf,jdf->sjcd", pre_grad, full_gate_up, preferred_element_type=jnp.float32
    ).astype(jnp.bfloat16)
    input_back = lax.all_to_all(input_grad, "expert", split_axis=0, concat_axis=0, tiled=True)
    input_pair = jnp.einsum(
        "tks,sd->td",
        select,
        input_back.reshape(slot_total, feature_dim),
        preferred_element_type=jnp.float32,
    )
    router_float = router.astype(jnp.float32)
    tokens_grad = (
        input_pair + jnp.dot(logit_grads, router_float.T, precision=lax.Precision.HIGHEST)
    ).astype(jnp.bfloat16)
    router_term = jnp.dot(
        tokens.astype(jnp.float32).T, logit_grads, precision=lax.Precision.HIGHEST
    )
    router_grad = lax.psum(router_term, ("dp", "expert"))
    gate_up_part = jnp.einsum(
        "sjcd,sjcf->jdf", received, pre_grad, preferred_element_type=jnp.float32
    )
    down_part = jnp.einsum("sjcf,sjcd->jfd", hidden, grad_recv, preferred_element_type=jnp.float32)
    gate_up_grad, down_grad = (
        lax.psum_scatter(
            gate_up_part.astype(jnp.bfloat16), "dp", scatter_dimension=1, tiled=True
        ).astype(jnp.float32),
        lax.psum_scatter(
            down_part.astype(jnp.bfloat16), "dp", scatter_dimension=1, tiled=True
        ).astype(jnp.float32),
    )
    return (mixed_out, tokens_grad, router_grad, gate_up_grad, down_grad)


def solution(mesh):
    placed = (
        P(("dp", "expert"), None),
        P(("dp", "expert"), None),
        P(),
        P("expert", "dp", None),
        P("expert", "dp", None),
        P(("dp", "expert"), None),
    )
    return jax.shard_map(
        on_device,
        mesh=mesh,
        in_specs=placed,
        out_specs=(
            P(("dp", "expert"), None),
            P(("dp", "expert"), None),
            P(),
            P("expert", "dp", None),
            P("expert", "dp", None),
        ),
        check_vma=False,
    )
```

profile of v0, /device:TPU:1, one launch (start us, length us, event | category | flops | bytes accessed | tf_op | source)
XLA Modules:
  0.0 444.5 jit_solution(6109489005997214316)
XLA Ops:
  7.2 0.7 all-gather.3.cloned.1.call-update
  8.0 0.7 all-gather.5.cloned.1.call-update
  9.8 1.6 convolution_convert_fusion
  11.4 6.5 %all-to-all-start = ((bf16[8,2,40,1024]{3,2,1,0:T(8,128)(2,1)}), bf16[8,2,40,1024]{3,2,1,0:T(8,128)(2,1)S(1)}, u32[]{:S(2)}, u32[]{:S(2)}) async-start(bf16[8,2,40,1024]{3,2,1,0:T(8,128)(2,1)} %bitcast.3), calls=%async_computation | async-start | bytes 2621440 | tf_op jit(solution)/shard_map/all_to_all | solution.py:55
  18.8 2.0 bitcast_convert_fusion.2
  20.8 28.3 %all-to-all-done = bf16[8,2,40,1024]{3,2,1,0:T(8,128)(2,1)S(1)} async-done(((bf16[8,2,40,1024]{3,2,1,0:T(8,128)(2,1)}), bf16[8,2,40,1024]{3,2,1,0:T(8,128)(2,1)S(1)}, u32[]{:S(2)}, u32[]{:S(2)}) %all-to-all-start) | async-done | bytes 1310752 | tf_op jit(solution)/shard_map/all_to_all | solution.py:55
  49.1 4.4 all-to-all-start.2
  53.6 45.8 %all-gather.3.cloned.1.call-done = bf16[2,1024,2048]{2,1,0:T(8,128)(2,1)} async-done(((bf16[2,256,2048]{2,1,0:T(8,128)(2,1)}), bf16[2,1024,2048]{2,1,0:T(8,128)(2,1)}) %all-gather.3.cloned.1.call-update) | async-done | bytes 8388624 | tf_op jit(solution)/shard_map/all_gather | solution.py:25
  99.3 8.1 %fusion.8 = f32[8,2,40,2048]{3,2,0,1:T(8,128)} fusion(bf16[2,1024,2048]{2,1,0:T(8,128)(2,1)} %all-gather.3.cloned.1.call-done, bf16[8,2,40,1024]{3,2,1,0:T(8,128)(2,1)S(1)} %all-to-all-done), kind=kOutput, calls=%fused_computation.10 | convolution fusion | flops 2684354560 | bytes 14942208 | tf_op jit(solution)/shard_map/sjcd,jdf->sjcf/dot_general | solution.py:56
  107.4 46.4 %all-gather.5.cloned.1.call-done = bf16[2,1024,1024]{2,1,0:T(8,128)(2,1)} async-done(((bf16[2,256,1024]{2,1,0:T(8,128)(2,1)}), bf16[2,1024,1024]{2,1,0:T(8,128)(2,1)}) %all-gather.5.cloned.1.call-update) | async-done | bytes 4194320 | tf_op jit(solution)/shard_map/all_gather | solution.py:26
  153.8 7.7 %fusion.13 = (bf16[8,2,40,1024]{3,2,0,1:T(8,128)(2,1)}, bf16[8,2,40,1024]{3,2,0,1:T(8,128)(2,1)}, bf16[8,2,40,1024]{3,2,0,1:T(8,128)(2,1)S(1)}) fusion(f32[8,2,40,2048]{3,2,0,1:T(8,128)} %fusion.8, bf16[2,1024,1024]{2,1,0:T(8,128)(2,1)} %all-gather.5.cloned.1.call-done, bf16[8,2,40,1024]{3,2,1,0:T(8,128)(2,1)S(1)} %all-to-all-done.2), kind=kOutput, calls=%fused_computation.16 | convolution fusion | flops 1352007680 | bytes 14680064 | tf_op jit(solution)/shard_map/sjcd,jfd->sjcf/dot_general | solution.py:76
  161.5 1.2 copy-done.7
  162.7 4.4 bitcast_convert_fusion.1
  167.1 1.2 copy-done.5
  168.4 8.1 %bitcast_convert_fusion = bf16[2,1024,2048]{2,1,0:T(8,128)(2,1)} fusion(bf16[8,2,40,1024]{3,2,1,0:T(8,128)(2,1)S(1)} %all-to-all-done, bf16[8,2,40,1024]{3,2,0,1:T(8,128)(2,1)} %get-tuple-element.10, bf16[8,2,40,1024]{3,2,0,1:T(8,128)(2,1)S(1)} %copy-done.5), kind=kOutput, calls=%fused_computation | convolution fusion | flops 2693791744 | bytes 12320768 | tf_op jit(solution)/shard_map/sjcd,sjcf->jdf/dot_general | solution.py:100
  176.5 1.3 copy-done.8
  177.8 3.7 fusion.26
  181.5 1.2 copy.38
  182.7 5.6 %all-to-all-start.1 = ((bf16[8,2,40,1024]{3,2,1,0:T(8,128)(2,1)}), bf16[8,2,40,1024]{3,2,1,0:T(8,128)(2,1)S(1)}, u32[]{:S(2)}, u32[]{:S(2)}) async-start(bf16[8,2,40,1024]{3,2,1,0:T(8,128)(2,1)} %copy.38), calls=%async_computation.1 | async-start | bytes 2621440 | tf_op jit(solution)/shard_map/all_to_all | solution.py:20
  188.2 6.9 %fusion.23 = bf16[8,2,40,1024]{3,2,0,1:T(8,128)(2,1)S(1)} fusion(bf16[2,1024,2048]{2,1,0:T(8,128)(2,1)} %all-gather.3.cloned.1.call-done, bf16[8,2,40,1024]{3,2,0,1:T(8,128)(2,1)} %get-tuple-element.10, bf16[8,2,40,1024]{3,2,0,1:T(8,128)(2,1)S(1)} %copy-done.6), kind=kOutput, calls=%fused_computation.26 | convolution fusion | flops 2690252800 | bytes 12320768 | tf_op jit(solution)/shard_map/sjcf,jdf->sjcd/dot_general | solution.py:82
  195.1 1.2 copy.40
  196.3 23.2 %all-to-all-done.1 = bf16[8,2,40,1024]{3,2,1,0:T(8,128)(2,1)S(1)} async-done(((bf16[8,2,40,1024]{3,2,1,0:T(8,128)(2,1)}), bf16[8,2,40,1024]{3,2,1,0:T(8,128)(2,1)S(1)}, u32[]{:S(2)}, u32[]{:S(2)}) %all-to-all-start.1) | async-done | bytes 1310752 | tf_op jit(solution)/shard_map/all_to_all | solution.py:20
  219.4 4.4 all-to-all-start.3
  224.1 2.8 multiply_reduce_fusion
  226.8 0.9 convolution_bitcast_fusion
  227.7 27.4 %all-to-all-done.3 = bf16[8,2,40,1024]{3,2,1,0:T(8,128)(2,1)S(1)} async-done(((bf16[8,2,40,1024]{3,2,1,0:T(8,128)(2,1)}), bf16[8,2,40,1024]{3,2,1,0:T(8,128)(2,1)S(1)}, u32[]{:S(2)}, u32[]{:S(2)}) %all-to-all-start.3) | async-done | bytes 1310752 | tf_op jit(solution)/shard_map/all_to_all | solution.py:85
  255.6 1.2 fusion.30
  256.8 2.8 convert_element_type.79
  259.6 49.5 %reduce-scatter.3.cloned.1.call-done = bf16[2,256,2048]{2,1,0:T(8,128)(2,1)} async-done(((bf16[2,1024,2048]{2,1,0:T(8,128)(2,1)}), bf16[2,256,2048]{2,1,0:T(8,128)(2,1)}) %reduce-scatter.3.cloned.1.call-update) | async-done | bytes 2097168 | tf_op jit(solution)/shard_map/reduce_scatter | solution.py:105
  309.1 4.1 convert_element_type.77
  313.2 123.3 %all-reduce.3.cloned.1.call-done = f32[1024,16]{0,1:T(8,128)} async-done(((f32[1024,16]{0,1:T(8,128)}), f32[1024,16]{0,1:T(8,128)}) %all-reduce.3.cloned.1.call-update) | async-done | bytes 65552 | tf_op jit(solution)/shard_map/psum | solution.py:99
  436.5 1.5 copy.61
  (45 shorter events, 2.7 us)
Async XLA Ops:
  7.2 2.6 copy-start
  7.2 1.5 copy-start.4
  7.2 92.2 %all-gather.3.cloned.1.call-start = ((), (), s32[]{:S(2)}) async-start(), calls=%async_computation.6 | async-start | bytes 10485760 | tf_op jit(solution)/shard_map/all_gather | solution.py:25
  7.9 145.9 %all-gather.5.cloned.1.call-start = ((), (), s32[]{:S(2)}) async-start(), calls=%async_computation.7 | async-start | bytes 5242880 | tf_op jit(solution)/shard_map/all_gather | solution.py:26
  11.4 6.5 %copy-start.2 = (bf16[160,1024]{1,0:T(8,128)(2,1)S(1)}, bf16[160,1024]{1,0:T(8,128)(2,1)}, u32[]{:S(2)}) copy-start(bf16[160,1024]{1,0:T(8,128)(2,1)} %param.11) | copy-start | bytes 983044
  11.4 6.6 %copy-start.3 = (bf16[1024,16]{0,1:T(8,128)(2,1)S(1)}, bf16[1024,16]{0,1:T(8,128)(2,1)}, u32[]{:S(2)}) copy-start(bf16[1024,16]{0,1:T(8,128)(2,1)} %param.8) | copy-start | bytes 98308
  11.4 37.7 %all-to-all-start = ((bf16[8,2,40,1024]{3,2,1,0:T(8,128)(2,1)}), bf16[8,2,40,1024]{3,2,1,0:T(8,128)(2,1)S(1)}, u32[]{:S(2)}, u32[]{:S(2)}) async-start(bf16[8,2,40,1024]{3,2,1,0:T(8,128)(2,1)} %bitcast.3), calls=%async_computation | async-start | bytes 2621440 | tf_op jit(solution)/shard_map/all_to_all | solution.py:55
  18.0 0.8 copy-start.1
  49.1 58.3 %all-to-all-start.2 = ((bf16[8,2,40,1024]{3,2,1,0:T(8,128)(2,1)}), bf16[8,2,40,1024]{3,2,1,0:T(8,128)(2,1)S(1)}, u32[]{:S(2)}, u32[]{:S(2)}) async-start(bf16[8,2,40,1024]{3,2,1,0:T(8,128)(2,1)} %bitcast.94), calls=%async_computation.2 | async-start | bytes 2621440 | tf_op jit(solution)/shard_map/all_to_all | solution.py:74
  53.6 203.2 %reduce-scatter.5.cloned.1.call-start = ((), (), s32[]{:S(2)}) async-start(), calls=%async_computation.10 | async-start | bytes 5242880 | tf_op jit(solution)/shard_map/reduce_scatter | solution.py:108
  161.5 1.2 copy-start.7
  167.1 1.3 copy-start.5
  167.1 142.0 %reduce-scatter.3.cloned.1.call-start = ((), (), s32[]{:S(2)}) async-start(), calls=%async_computation.9 | async-start | bytes 10485760 | tf_op jit(solution)/shard_map/reduce_scatter | solution.py:105
  176.5 1.3 copy-start.8
  182.7 5.6 %copy-start.6 = (bf16[8,2,40,1024]{3,2,0,1:T(8,128)(2,1)S(1)}, bf16[8,2,40,1024]{3,2,0,1:T(8,128)(2,1)}, u32[]{:S(2)}) copy-start(bf16[8,2,40,1024]{3,2,0,1:T(8,128)(2,1)} %get-tuple-element.9) | copy-start | bytes 3932164
  182.7 36.8 %all-to-all-start.1 = ((bf16[8,2,40,1024]{3,2,1,0:T(8,128)(2,1)}), bf16[8,2,40,1024]{3,2,1,0:T(8,128)(2,1)S(1)}, u32[]{:S(2)}, u32[]{:S(2)}) async-start(bf16[8,2,40,1024]{3,2,1,0:T(8,128)(2,1)} %copy.38), calls=%async_computation.1 | async-start | bytes 2621440 | tf_op jit(solution)/shard_map/all_to_all | solution.py:20
  219.4 35.7 %all-to-all-start.3 = ((bf16[8,2,40,1024]{3,2,1,0:T(8,128)(2,1)}), bf16[8,2,40,1024]{3,2,1,0:T(8,128)(2,1)S(1)}, u32[]{:S(2)}, u32[]{:S(2)}) async-start(bf16[8,2,40,1024]{3,2,1,0:T(8,128)(2,1)} %copy.40), calls=%async_computation.3 | async-start | bytes 2621440 | tf_op jit(solution)/shard_map/all_to_all | solution.py:85
  223.9 212.7 %all-reduce.3.cloned.1.call-start = ((), (), s32[]{:S(2)}) async-start(), calls=%async_computation.8 | async-start | bytes 131072 | tf_op jit(solution)/shard_map/psum | solution.py:99
Sparse Core Ops, SparseCore 0:
  9.8 89.4 all-gather.2
  101.2 52.5 all-gather.4
  167.2 52.5 reduce-scatter.4
  222.7 86.3 reduce-scatter.2
  315.1 121.4 all-reduce.2
where the time goes:
time: 445 us
  waiting for transfers between devices  345 us (78%)
  matrix products  47.9 us (11%)
  starting transfers between devices  21.1 us (5%)
  between operations  13.9 us (3%)
  local copies, waits for them, and re-layouts  8.27 us (2%)
  other arithmetic  8.07 us (2%)
    psum x1, waiting for transfers between devices, on_device(): router_grad = lax.psum(router_term, ('dp', 'expert'))  123 us
    reduce_scatter x1, waiting for transfers between devices, on_device(): lax.psum_scatter(gate_up_part.astype(jnp.bfloat16), 'dp', scatter_dimensi...  49.5 us
    all_gather x1, waiting for transfers between devices, on_device(): lax.all_gather(down_weight, 'dp', axis=1, tiled=True)  46.4 us
    all_gather x1, waiting for transfers between devices, on_device(): lax.all_gather(gate_up_weight, 'dp', axis=1, tiled=True)  45.8 us
    all_to_all x1, waiting for transfers between devices, on_device(): lax.all_to_all(send_rows, 'expert', split_axis=0, concat_axis=0, tiled=True)  28.3 us
    all_to_all x1, waiting for transfers between devices, on_device(): lax.all_to_all(input_grad, 'expert', split_axis=0, concat_axis=0, tiled=T...  27.4 us
    all_to_all x1, waiting for transfers between devices, finish_rows(): lax.all_to_all(produced, 'expert', split_axis=0, concat_axis=0, tiled=True)  23.2 us
  transfers between devices with their start and end apart: 9, of which 7 were waited for; matrix products, arithmetic and copies ran while one was open for 10% of the time, Pallas kernels for 0%

commit v1 on v0

--- a/solution.py
+++ b/solution.py
@@ -96,7 +96,9 @@
     router_term = jnp.dot(
         tokens.astype(jnp.float32).T, logit_grads, precision=lax.Precision.HIGHEST
     )
-    router_grad = lax.psum(router_term, ("dp", "expert"))
+    router_grad = router_term
+    for name in ("expert", "dp"):
+        router_grad = lax.psum(router_grad, name)
     gate_up_part = jnp.einsum(
         "sjcd,sjcf->jdf", received, pre_grad, preferred_element_type=jnp.float32
     )

time: 445 us -> 462 us (1.038)
  waiting for transfers between devices: 345 us -> 362 us
    psum x1 -> x2, waiting for transfers between devices: 123 us -> 40.2 us  [on_device(): router_grad = lax.psum(router_grad, name)]
    reduce_scatter x1, waiting for transfers between devices: 0.01 us -> 50.6 us  [on_device(): lax.psum_scatter(down_part.astype(jnp.bfloat16), 'dp', scatter_dimension=...]
    reduce_scatter x1, waiting for transfers between devices: 49.5 us -> 86.5 us  [on_device(): lax.psum_scatter(gate_up_part.astype(jnp.bfloat16), 'dp', scatter_dimensi...]
    all_to_all x1, waiting for transfers between devices: 23.2 us -> 31.3 us  [finish_rows(): lax.all_to_all(produced, 'expert', split_axis=0, concat_axis=0, tiled=True)]
  transfers between devices with their start and end apart: 9 -> 10, of which waited for: 7 -> 8; matrix products, arithmetic and copies ran while one was open for 10% -> 9% of each run, Pallas kernels for 0% -> 0%
where the time goes in v1:
time: 462 us; the launch traced here: 460 us
  waiting for transfers between devices  362 us (78%)
  matrix products  47.4 us (10%)
  starting transfers between devices  21.2 us (5%)
  between operations  14.3 us (3%)
  other arithmetic  8.07 us (2%)
  local copies, waits for them, and re-layouts  6.97 us (2%)
    reduce_scatter x1, waiting for transfers between devices, on_device(): lax.psum_scatter(gate_up_part.astype(jnp.bfloat16), 'dp', scatter_dimensi...  86.5 us
    reduce_scatter x1, waiting for transfers between devices, on_device(): lax.psum_scatter(down_part.astype(jnp.bfloat16), 'dp', scatter_dimension=...  50.6 us
    all_gather x1, waiting for transfers between devices, on_device(): lax.all_gather(down_weight, 'dp', axis=1, tiled=True)  46.4 us
    all_gather x1, waiting for transfers between devices, on_device(): lax.all_gather(gate_up_weight, 'dp', axis=1, tiled=True)  45.8 us
    psum x2, waiting for transfers between devices, on_device(): router_grad = lax.psum(router_grad, name)  40.2 us
    all_to_all x1, waiting for transfers between devices, on_device(): lax.all_to_all(input_grad, 'expert', split_axis=0, concat_axis=0, tiled=T...  31.7 us
    all_to_all x1, waiting for transfers between devices, finish_rows(): lax.all_to_all(produced, 'expert', split_axis=0, concat_axis=0, tiled=True)  31.3 us
    all_to_all x1, waiting for transfers between devices, on_device(): lax.all_to_all(send_rows, 'expert', split_axis=0, concat_axis=0, tiled=True)  28.2 us
  transfers between devices with their start and end apart: 10, of which 8 were waited for; matrix products, arithmetic and copies ran while one was open for 9% of the time, Pallas kernels for 0%

profile of v1, /device:TPU:1, one launch (start us, length us, event | category | flops | bytes accessed | tf_op | source)
XLA Modules:
  0.0 460.0 jit_solution(11968571833887685165)
XLA Ops:
  7.2 0.7 all-gather.3.cloned.1.call-update
  8.0 0.7 all-gather.5.cloned.1.call-update
  9.8 1.6 convolution_convert_fusion
  11.4 6.5 %all-to-all-start = ((bf16[8,2,40,1024]{3,2,1,0:T(8,128)(2,1)}), bf16[8,2,40,1024]{3,2,1,0:T(8,128)(2,1)S(1)}, u32[]{:S(2)}, u32[]{:S(2)}) async-start(bf16[8,2,40,1024]{3,2,1,0:T(8,128)(2,1)} %bitcast.3), calls=%async_computation | async-start | bytes 2621440 | tf_op jit(solution)/shard_map/all_to_all | solution.py:55
  18.8 2.0 bitcast_convert_fusion.2
  20.9 28.2 %all-to-all-done = bf16[8,2,40,1024]{3,2,1,0:T(8,128)(2,1)S(1)} async-done(((bf16[8,2,40,1024]{3,2,1,0:T(8,128)(2,1)}), bf16[8,2,40,1024]{3,2,1,0:T(8,128)(2,1)S(1)}, u32[]{:S(2)}, u32[]{:S(2)}) %all-to-all-start) | async-done | bytes 1310752 | tf_op jit(solution)/shard_map/all_to_all | solution.py:55
  49.1 4.4 all-to-all-start.2
  53.6 45.8 %all-gather.3.cloned.1.call-done = bf16[2,1024,2048]{2,1,0:T(8,128)(2,1)} async-done(((bf16[2,256,2048]{2,1,0:T(8,128)(2,1)}), bf16[2,1024,2048]{2,1,0:T(8,128)(2,1)}) %all-gather.3.cloned.1.call-update) | async-done | bytes 8388624 | tf_op jit(solution)/shard_map/all_gather | solution.py:25
  99.3 8.0 %fusion.8 = f32[8,2,40,2048]{3,2,0,1:T(8,128)} fusion(bf16[2,1024,2048]{2,1,0:T(8,128)(2,1)} %all-gather.3.cloned.1.call-done, bf16[8,2,40,1024]{3,2,1,0:T(8,128)(2,1)S(1)} %all-to-all-done), kind=kOutput, calls=%fused_computation.10 | convolution fusion | flops 2684354560 | bytes 14942208 | tf_op jit(solution)/shard_map/sjcd,jdf->sjcf/dot_general | solution.py:56
  107.4 46.4 %all-gather.5.cloned.1.call-done = bf16[2,1024,1024]{2,1,0:T(8,128)(2,1)} async-done(((bf16[2,256,1024]{2,1,0:T(8,128)(2,1)}), bf16[2,1024,1024]{2,1,0:T(8,128)(2,1)}) %all-gather.5.cloned.1.call-update) | async-done | bytes 4194320 | tf_op jit(solution)/shard_map/all_gather | solution.py:26
  153.8 8.2 %fusion.13 = (bf16[8,2,40,1024]{3,2,0,1:T(8,128)(2,1)}, bf16[8,2,40,1024]{3,2,0,1:T(8,128)(2,1)}, bf16[8,2,40,1024]{3,2,0,1:T(8,128)(2,1)S(1)}) fusion(f32[8,2,40,2048]{3,2,0,1:T(8,128)} %fusion.8, bf16[2,1024,1024]{2,1,0:T(8,128)(2,1)} %all-gather.5.cloned.1.call-done, bf16[8,2,40,1024]{3,2,1,0:T(8,128)(2,1)S(1)} %all-to-all-done.2), kind=kOutput, calls=%fused_computation.16 | convolution fusion | flops 1352007680 | bytes 14680064 | tf_op jit(solution)/shard_map/sjcd,jfd->sjcf/dot_general | solution.py:76
  162.0 1.5 fusion.26
  163.5 1.2 copy.38
  164.7 5.4 %all-to-all-start.1 = ((bf16[8,2,40,1024]{3,2,1,0:T(8,128)(2,1)}), bf16[8,2,40,1024]{3,2,1,0:T(8,128)(2,1)}, u32[]{:S(2)}, u32[]{:S(2)}) async-start(bf16[8,2,40,1024]{3,2,1,0:T(8,128)(2,1)} %copy.38), calls=%async_computation.1 | async-start | bytes 2621440 | tf_op jit(solution)/shard_map/all_to_all | solution.py:20
  170.2 31.3 %all-to-all-done.1 = bf16[8,2,40,1024]{3,2,1,0:T(8,128)(2,1)} async-done(((bf16[8,2,40,1024]{3,2,1,0:T(8,128)(2,1)}), bf16[8,2,40,1024]{3,2,1,0:T(8,128)(2,1)}, u32[]{:S(2)}, u32[]{:S(2)}) %all-to-all-start.1) | async-done | bytes 1310752 | tf_op jit(solution)/shard_map/all_to_all | solution.py:20
  201.5 3.1 multiply_reduce_fusion
  204.6 0.9 convolution_bitcast_fusion
  205.6 5.7 %bitcast_convert_fusion.1 = bf16[2,1024,1024]{2,1,0:T(8,128)(2,1)} fusion(bf16[8,2,40,1024]{3,2,0,1:T(8,128)(2,1)} %copy-done.8, bf16[8,2,40,1024]{3,2,1,0:T(8,128)(2,1)S(1)} %all-to-all-done.2), kind=kOutput, calls=%fused_computation.1 | convolution fusion | flops 1344274432 | bytes 6815744 | tf_op jit(solution)/shard_map/sjcf,sjcd->jfd/dot_general | solution.py:105
  211.5 1.1 copy-done.6
  212.6 8.1 %bitcast_convert_fusion = bf16[2,1024,2048]{2,1,0:T(8,128)(2,1)} fusion(bf16[8,2,40,1024]{3,2,1,0:T(8,128)(2,1)S(1)} %all-to-all-done, bf16[8,2,40,1024]{3,2,0,1:T(8,128)(2,1)} %get-tuple-element.10, bf16[8,2,40,1024]{3,2,0,1:T(8,128)(2,1)S(1)} %copy-done.6), kind=kOutput, calls=%fused_computation | convolution fusion | flops 2693791744 | bytes 12320768 | tf_op jit(solution)/shard_map/sjcd,sjcf->jdf/dot_general | solution.py:102
  220.7 1.3 copy-done.7
  222.0 6.3 %fusion.23 = bf16[8,2,40,1024]{3,2,0,1:T(8,128)(2,1)S(1)} fusion(bf16[2,1024,2048]{2,1,0:T(8,128)(2,1)} %all-gather.3.cloned.1.call-done, bf16[8,2,40,1024]{3,2,0,1:T(8,128)(2,1)S(1)} %copy-done.7, bf16[8,2,40,1024]{3,2,0,1:T(8,128)(2,1)S(1)} %copy-done.6), kind=kOutput, calls=%fused_computation.26 | convolution fusion | flops 2690252800 | bytes 12320768 | tf_op jit(solution)/shard_map/sjcf,jdf->sjcd/dot_general | solution.py:82
  228.3 1.2 copy.40
  229.5 4.4 all-to-all-start.3
  234.1 31.7 %all-to-all-done.3 = bf16[8,2,40,1024]{3,2,1,0:T(8,128)(2,1)S(1)} async-done(((bf16[8,2,40,1024]{3,2,1,0:T(8,128)(2,1)}), bf16[8,2,40,1024]{3,2,1,0:T(8,128)(2,1)S(1)}, u32[]{:S(2)}, u32[]{:S(2)}) %all-to-all-start.3) | async-done | bytes 1310752 | tf_op jit(solution)/shard_map/all_to_all | solution.py:85
  266.3 1.2 fusion.30
  267.5 50.6 %reduce-scatter.5.cloned.1.call-done = bf16[2,256,1024]{2,1,0:T(8,128)(2,1)} async-done(((bf16[2,1024,1024]{2,1,0:T(8,128)(2,1)}), bf16[2,256,1024]{2,1,0:T(8,128)(2,1)}) %reduce-scatter.5.cloned.1.call-update) | async-done | bytes 1048592 | tf_op jit(solution)/shard_map/reduce_scatter | solution.py:110
  318.1 2.8 convert_element_type.79
  320.9 86.5 %reduce-scatter.3.cloned.1.call-done = bf16[2,256,2048]{2,1,0:T(8,128)(2,1)} async-done(((bf16[2,1024,2048]{2,1,0:T(8,128)(2,1)}), bf16[2,256,2048]{2,1,0:T(8,128)(2,1)}) %reduce-scatter.3.cloned.1.call-update) | async-done | bytes 2097168 | tf_op jit(solution)/shard_map/reduce_scatter | solution.py:107
  407.4 4.1 convert_element_type.77
  411.5 40.2 %all-reduce.6.cloned.1.call-done = f32[1024,16]{0,1:T(8,128)} async-done(((f32[1024,16]{0,1:T(8,128)}), f32[1024,16]{0,1:T(8,128)}) %all-reduce.6.cloned.1.call-update) | async-done | bytes 65552 | tf_op jit(solution)/shard_map/psum | solution.py:101
  451.7 1.5 copy.62
  (48 shorter events, 3.0 us)
Async XLA Ops:
  7.2 2.6 copy-start
  7.2 1.5 copy-start.4
  7.2 92.2 %all-gather.3.cloned.1.call-start = ((), (), s32[]{:S(2)}) async-start(), calls=%async_computation.6 | async-start | bytes 10485760 | tf_op jit(solution)/shard_map/all_gather | solution.py:25
  7.9 145.9 %all-gather.5.cloned.1.call-start = ((), (), s32[]{:S(2)}) async-start(), calls=%async_computation.7 | async-start | bytes 5242880 | tf_op jit(solution)/shard_map/all_gather | solution.py:26
  11.4 6.5 %copy-start.2 = (bf16[160,1024]{1,0:T(8,128)(2,1)S(1)}, bf16[160,1024]{1,0:T(8,128)(2,1)}, u32[]{:S(2)}) copy-start(bf16[160,1024]{1,0:T(8,128)(2,1)} %param.11) | copy-start | bytes 983044
  11.4 6.6 %copy-start.3 = (bf16[1024,16]{0,1:T(8,128)(2,1)S(1)}, bf16[1024,16]{0,1:T(8,128)(2,1)}, u32[]{:S(2)}) copy-start(bf16[1024,16]{0,1:T(8,128)(2,1)} %param.8) | copy-start | bytes 98308
  11.4 37.7 %all-to-all-start = ((bf16[8,2,40,1024]{3,2,1,0:T(8,128)(2,1)}), bf16[8,2,40,1024]{3,2,1,0:T(8,128)(2,1)S(1)}, u32[]{:S(2)}, u32[]{:S(2)}) async-start(bf16[8,2,40,1024]{3,2,1,0:T(8,128)(2,1)} %bitcast.3), calls=%async_computation | async-start | bytes 2621440 | tf_op jit(solution)/shard_map/all_to_all | solution.py:55
  18.0 0.9 copy-start.1
  49.1 58.3 %all-to-all-start.2 = ((bf16[8,2,40,1024]{3,2,1,0:T(8,128)(2,1)}), bf16[8,2,40,1024]{3,2,1,0:T(8,128)(2,1)S(1)}, u32[]{:S(2)}, u32[]{:S(2)}) async-start(bf16[8,2,40,1024]{3,2,1,0:T(8,128)(2,1)} %bitcast.93), calls=%async_computation.2 | async-start | bytes 2621440 | tf_op jit(solution)/shard_map/all_to_all | solution.py:74
  153.8 8.2 %copy-start.5 = (bf16[2,1024,1024]{2,1,0:T(8,128)(2,1)S(1)}, bf16[2,1024,1024]{2,1,0:T(8,128)(2,1)}, u32[]{:S(2)}) copy-start(bf16[2,1024,1024]{2,1,0:T(8,128)(2,1)} %all-gather.5.cloned.1.call-done) | copy-start | bytes 12582916
  162.0 1.5 copy-start.8
  164.7 36.8 %all-to-all-start.1 = ((bf16[8,2,40,1024]{3,2,1,0:T(8,128)(2,1)}), bf16[8,2,40,1024]{3,2,1,0:T(8,128)(2,1)}, u32[]{:S(2)}, u32[]{:S(2)}) async-start(bf16[8,2,40,1024]{3,2,1,0:T(8,128)(2,1)} %copy.38), calls=%async_computation.1 | async-start | bytes 2621440 | tf_op jit(solution)/shard_map/all_to_all | solution.py:20
  170.1 96.1 %all-reduce.4.cloned.1.call-start = ((), (), s32[]{:S(2)}) async-start(), calls=%async_computation.8 | async-start | bytes 131072 | tf_op jit(solution)/shard_map/psum | solution.py:101
  205.5 112.6 %reduce-scatter.5.cloned.1.call-start = ((), (), s32[]{:S(2)}) async-start(), calls=%async_computation.11 | async-start | bytes 5242880 | tf_op jit(solution)/shard_map/reduce_scatter | solution.py:110
  211.3 1.3 copy-start.6
  211.3 196.1 %reduce-scatter.3.cloned.1.call-start = ((), (), s32[]{:S(2)}) async-start(), calls=%async_computation.10 | async-start | bytes 10485760 | tf_op jit(solution)/shard_map/reduce_scatter | solution.py:107
  220.7 1.3 copy-start.7
  229.5 36.3 %all-to-all-start.3 = ((bf16[8,2,40,1024]{3,2,1,0:T(8,128)(2,1)}), bf16[8,2,40,1024]{3,2,1,0:T(8,128)(2,1)S(1)}, u32[]{:S(2)}, u32[]{:S(2)}) async-start(bf16[8,2,40,1024]{3,2,1,0:T(8,128)(2,1)} %copy.40), calls=%async_computation.3 | async-start | bytes 2621440 | tf_op jit(solution)/shard_map/all_to_all | solution.py:85
  233.9 217.8 %all-reduce.6.cloned.1.call-start = ((), (), s32[]{:S(2)}) async-start(), calls=%async_computation.9 | async-start | bytes 131072 | tf_op jit(solution)/shard_map/psum | solution.py:101
Sparse Core Ops, SparseCore 0:
  9.8 89.4 all-gather.2
  101.2 52.5 all-gather.4
  205.6 54.3 all-reduce.3
  263.4 54.6 reduce-scatter.4
  321.0 86.3 reduce-scatter.2
  410.1 41.5 all-reduce.5
